TPU v7x, 32 devices: a whole 2x2x4 slice. The times are simulated.
32 devices in a mesh: facet: 4 (over y, x), band: 4 (over z), sub: 2 (over core).
Axes of the slice: x: 2, y: 2, z: 4, core: 2. Of those that a mesh axis runs over, the one named last changes fastest.
Arguments:
- facets: bfloat16 [8192, 2048], P(('facet', 'band')), may hold values from -6 to 6
- window: float32 [2048], replicated, may hold values from 0.5 to 1.5
- facet_offsets: int32 [4, 2], replicated, may hold values from 0 to 49151
- row_offsets: int32 [8], replicated, may hold values from 0 to 49151
- column_offset: int32 [1], replicated, may hold values from 0 to 49151
- kernel: bfloat16 [256, 256], replicated, may hold values from -0.375 to 0.375
- tile_counts: int32 [8, 16, 16], replicated, may hold values from 0 to 32
Outputs:
- residual: bfloat16 [8192, 2048], P(('facet', 'band'))
All inputs are finite; a program needn't handle non-finite values.
Results may differ from a plain program's by a relative error of at most 0.013.
Values may be sent and summed in bfloat16 or wider, within the bound.
A program may use at most 64 MiB of HBM per device.

v0:
```python
import math
import jax
import jax.numpy as jnp
from jax import lax
from jax.sharding import PartitionSpec as P

IMAGE = 49152


def modular_product(first, second):
    upper_bits = first // 256
    lower_bits = first % 256
    reduced = upper_bits * second % IMAGE
    reduced = reduced * 256 % IMAGE
    return (reduced + lower_bits * second) % IMAGE


def phase_table(frequency, position):
    reduced = modular_product(frequency % IMAGE, position % IMAGE)
    angle = reduced.astype(jnp.float32) * (2.0 * math.pi / IMAGE)
    return (jnp.cos(angle), jnp.sin(angle))


def product(left, right):
    return jnp.dot(left, right, preferred_element_type=jnp.float32)


def body(facets, window, facet_offsets, row_offsets, column_offset, kernel, tile_counts):
    facet_count = lax.axis_size("facet")
    band_count = lax.axis_size("band")
    sub_count = lax.axis_size("sub")
    facet_at = lax.axis_index("facet")
    band_at = lax.axis_index("band")
    sub_at = lax.axis_index("sub")
    band_rows = facets.shape[0]
    width = facets.shape[1]
    contrib = kernel.shape[0]
    sub_rows = contrib // band_count
    stacked = band_count * contrib
    a_scale = 1.0 / math.sqrt(width * facet_count)
    b_scale = 1.0 / math.sqrt(width)
    back_scale = 1.0 / math.sqrt(band_count * sub_count * contrib)
    out_scale = 1.0 / math.sqrt(contrib)
    offset = lax.dynamic_slice_in_dim(facet_offsets, facet_at, 1, 0)[0]
    cells = jnp.arange(width, dtype=jnp.int32)
    frequencies = jnp.arange(contrib, dtype=jnp.int32)
    cosine, sine = phase_table(column_offset[0] + frequencies[:, None], offset[1] + cells[None, :])
    col_real = (cosine * window[None, :] * b_scale).astype(jnp.bfloat16)
    col_imag = (-sine * window[None, :] * b_scale).astype(jnp.bfloat16)
    t_real = jnp.einsum("xy,ky->xk", facets, col_real, preferred_element_type=jnp.float32).astype(
        jnp.bfloat16
    )
    t_imag = jnp.einsum("xy,ky->xk", facets, col_imag, preferred_element_type=jnp.float32).astype(
        jnp.bfloat16
    )
    starts = lax.dynamic_slice_in_dim(row_offsets, sub_at * band_count, band_count, 0)
    row_freqs = (starts[:, None] + frequencies[None, :]).reshape(stacked)
    positions = offset[0] + band_at * band_rows + jnp.arange(band_rows, dtype=jnp.int32)
    row_cos, row_sin = phase_table(row_freqs[:, None], positions[None, :])
    a_real = (row_cos * a_scale).astype(jnp.bfloat16)
    a_imag = (-row_sin * a_scale).astype(jnp.bfloat16)
    part_real = product(a_real, t_real) - product(a_imag, t_imag)
    part_imag = product(a_real, t_imag) + product(a_imag, t_real)
    terms = jnp.stack([part_real, part_imag]).reshape(2, band_count, band_count, sub_rows, contrib)
    blocks = lax.psum_scatter(
        terms.astype(jnp.bfloat16), "band", scatter_dimension=2, tiled=True
    ).astype(jnp.float32)
    blocks = lax.psum(blocks, "facet")
    grid_part = blocks.reshape(2, band_count, sub_rows, contrib).astype(jnp.bfloat16)
    tiles = tile_counts.shape[1]
    tile_side = contrib // tiles
    counts = lax.dynamic_slice_in_dim(tile_counts, sub_at * band_count, band_count, 0).astype(
        jnp.float32
    )
    ratio = counts / (counts + 4.0)
    weights = jnp.broadcast_to(
        ratio[:, :, None, :, None], (band_count, tiles, tile_side, tiles, tile_side)
    )
    weights = weights.reshape(band_count, contrib, contrib)
    y_cols = jnp.einsum(
        "ij,cgrj->cgir", kernel, grid_part, preferred_element_type=jnp.float32
    ).astype(jnp.bfloat16)
    y_cols = lax.all_to_all(y_cols, "band", split_axis=2, concat_axis=3, tiled=True)
    z_cols = jnp.einsum("cgqi,ji->cgqj", y_cols, kernel, preferred_element_type=jnp.float32)
    weight_cols = jnp.swapaxes(
        lax.dynamic_slice_in_dim(weights, band_at * sub_rows, sub_rows, 2), 1, 2
    )
    w_cols = (weight_cols[None] * z_cols).astype(jnp.bfloat16)
    u_cols = jnp.einsum("cgqj,jl->cgql", w_cols, kernel, preferred_element_type=jnp.float32).astype(
        jnp.bfloat16
    )
    u_back = lax.all_to_all(u_cols, "band", split_axis=3, concat_axis=2, tiled=True)
    residual_grid = jnp.einsum(
        "cgqr,qm->cgrm", u_back, kernel, preferred_element_type=jnp.float32
    ).astype(jnp.bfloat16)
    back_real = (row_cos * back_scale).astype(jnp.bfloat16).reshape(band_count, contrib, band_rows)
    back_imag = (row_sin * back_scale).astype(jnp.bfloat16).reshape(band_count, contrib, band_rows)
    piece = lax.all_gather(residual_grid, "band", axis=2, tiled=True)
    e_real = jnp.einsum("gkx,gkl->xl", back_real, piece[0], preferred_element_type=jnp.float32)
    e_real = e_real - jnp.einsum(
        "gkx,gkl->xl", back_imag, piece[1], preferred_element_type=jnp.float32
    )
    e_imag = jnp.einsum("gkx,gkl->xl", back_real, piece[1], preferred_element_type=jnp.float32)
    e_imag = e_imag + jnp.einsum(
        "gkx,gkl->xl", back_imag, piece[0], preferred_element_type=jnp.float32
    )
    e_real, e_imag = (e_real, e_imag)
    e_real, e_imag = (
        lax.psum(e_real.astype(jnp.bfloat16), "sub").astype(jnp.float32),
        lax.psum(e_imag.astype(jnp.bfloat16), "sub").astype(jnp.float32),
    )
    out_cos = (cosine * out_scale).astype(jnp.bfloat16)
    out_sin = (sine * out_scale).astype(jnp.bfloat16)
    image = product(e_real.astype(jnp.bfloat16), out_cos) - product(
        e_imag.astype(jnp.bfloat16), out_sin
    )
    return (window[None, :] * image).astype(jnp.bfloat16)


def solution(mesh):
    in_specs = (P(("facet", "band"), None), P(), P(), P(), P(), P(), P())
    out_specs = P(("facet", "band"), None)
    return jax.shard_map(body, mesh=mesh, in_specs=in_specs, out_specs=out_specs, check_vma=False)
```

profile of v0, /device:TPU:0, one launch (start us, length us, event | category | flops | bytes accessed | tf_op | source)
XLA Modules:
  0.0 311.3 jit_solution(18280598410825204298)
XLA Ops:
  7.3 0.8 constant_dynamic-slice_fusion
  8.1 0.5 fusion.138
  8.7 0.7 add_select_fusion.9
  9.3 12.9 %convolution_convert_fusion.3 = bf16[256,512]{1,0:T(8,128)(2,1)} fusion(bf16[512,2048]{1,0:T(8,128)(2,1)S(1)} %copy-done, f32[2048]{0:T(1024)} %param.8, s32[256]{0:T(256)S(1)} %get-tuple-element.14, s32[2048]{0:T(1024)S(1)} %add_select_fusion.9, s32[256]{0:T(256)S(1)} %get-tuple-element.15), kind=kOutput, calls=%fused_computation.73 | convolution fusion | flops 551682048 | bytes 2377728 | tf_op jit(solution)/shard_map/xy,ky->xk/dot_general | solution.py:53
  22.3 10.5 %convolution_convert_fusion.4 = bf16[256,512]{1,0:T(8,128)(2,1)S(1)} fusion(bf16[512,2048]{1,0:T(8,128)(2,1)S(1)} %copy-done, f32[2048]{0:T(1024)S(1)} %copy-done.11, s32[256]{0:T(256)S(1)} %get-tuple-element.14, s32[2048]{0:T(1024)S(1)} %add_select_fusion.9, s32[256]{0:T(256)S(1)} %get-tuple-element.15), kind=kOutput, calls=%fused_computation.74 | convolution fusion | flops 551157760 | bytes 2377728 | tf_op jit(solution)/shard_map/xy,ky->xk/dot_general | solution.py:50
  33.6 10.6 %fusion.58 = f32[1024,256]{1,0:T(8,128)S(1)} fusion(bf16[256,512]{1,0:T(8,128)(2,1)S(1)} %convolution_convert_fusion.4, s32[1024]{0:T(1024)S(1)} %get-tuple-element.8, s32[512]{0:T(512)S(1)} %add_select_fusion.16, s32[1024]{0:T(1024)S(1)} %get-tuple-element.7), kind=kOutput, calls=%fused_computation.88 | convolution fusion | flops 282066944 | bytes 1320960 | tf_op jit(solution)/shard_map/dot_general | solution.py:25
  44.2 10.7 %fusion.57 = f32[1024,256]{1,0:T(8,128)S(1)} fusion(bf16[256,512]{1,0:T(8,128)(2,1)S(1)} %copy-done.14, s32[1024]{0:T(1024)S(1)} %get-tuple-element.8, s32[512]{0:T(512)S(1)} %add_select_fusion.16, s32[1024]{0:T(1024)S(1)} %get-tuple-element.7), kind=kOutput, calls=%fused_computation.87 | convolution fusion | flops 282066944 | bytes 1320960 | tf_op jit(solution)/shard_map/dot_general | solution.py:25
  54.9 11.6 %fusion.36 = bf16[1024,256]{1,0:T(8,128)(2,1)S(1)} fusion(f32[1024,256]{1,0:T(8,128)S(1)} %fusion.58, bf16[256,512]{1,0:T(8,128)(2,1)S(1)} %copy-done.14, s32[1024]{0:T(1024)S(1)} %get-tuple-element.8, s32[512]{0:T(512)S(1)} %add_select_fusion.16, s32[1024]{0:T(1024)S(1)} %get-tuple-element.7), kind=kOutput, calls=%fused_computation.59 | convolution fusion | flops 283115520 | bytes 1845248 | tf_op jit(solution)/shard_map/dot_general | solution.py:25
  66.5 12.0 %fusion.37 = bf16[1024,256]{1,0:T(8,128)(2,1)S(1)} fusion(f32[1024,256]{1,0:T(8,128)S(1)} %fusion.57, bf16[256,512]{1,0:T(8,128)(2,1)S(1)} %convolution_convert_fusion.4, s32[1024]{0:T(1024)S(1)} %get-tuple-element.8, s32[512]{0:T(512)S(1)} %add_select_fusion.16, s32[1024]{0:T(1024)S(1)} %get-tuple-element.7), kind=kOutput, calls=%fused_computation.60 | convolution fusion | flops 283115520 | bytes 1845248 | tf_op jit(solution)/shard_map/dot_general | solution.py:25
  78.6 1.0 copy.25
  79.8 30.1 %reduce-scatter.2.cloned.1.call-done = bf16[2,4,1,64,256]{4,3,1,0,2:T(8,128)(2,1)} async-done(((bf16[2,4,4,64,256]{4,3,1,0,2:T(8,128)(2,1)}), bf16[2,4,1,64,256]{4,3,1,0,2:T(8,128)(2,1)}) %reduce-scatter.2.cloned.1.call-update) | async-done | bytes 262160 | tf_op jit(solution)/shard_map/reduce_scatter | solution.py:65
  109.9 44.5 %all-reduce.4.cloned.1.call-done = bf16[2,4,1,64,256]{4,3,1,0,2:T(8,128)(2,1)} async-done(((bf16[2,4,1,64,256]{4,3,1,0,2:T(8,128)(2,1)}), bf16[2,4,1,64,256]{4,3,1,0,2:T(8,128)(2,1)}) %all-reduce.4.cloned.1.call-update) | async-done | bytes 262160 | tf_op jit(solution)/shard_map/psum | solution.py:68
  154.4 1.2 fusion.43
  155.9 1.1 reshape.290
  157.0 4.6 %all-to-all-start = ((bf16[4,2,16384]{2,1,0:T(2,128)(2,1)}), bf16[4,2,16384]{2,1,0:T(2,128)(2,1)S(1)}, u32[]{:S(2)}, u32[]{:S(2)}) async-start(bf16[4,2,16384]{2,1,0:T(2,128)(2,1)} %reshape.290), calls=%async_computation.1 | async-start | bytes 524288 | tf_op jit(solution)/shard_map/all_to_all | solution.py:83
  161.7 3.9 %broadcast_in_dim.2 = f32[4,16,16,16,16]{2,1,4,3,0:T(8,128)} broadcast(f32[4,16,16]{1,2,0:T(8,128)S(1)} %copy.17), dimensions={0,1,3} | broadcast | bytes 1052672 | tf_op jit(solution)/shard_map/broadcast_in_dim | solution.py:76
  165.6 6.1 %reshape.284 = f32[4,256,256]{1,2,0:T(8,128)S(1)} reshape(f32[4,16,16,16,16]{2,1,4,3,0:T(8,128)} %broadcast_in_dim.2) | data formatting | bytes 2097152 | tf_op jit(solution)/shard_map/reshape | solution.py:79
  171.7 0.7 dynamic-slice_bitcast_fusion
  172.8 0.4 copy.30
  173.6 1.4 convolution_convert_fusion.1
  175.3 0.4 reshape.292
  175.7 12.7 %all_to_all.36 = bf16[4,2,16384]{2,1,0:T(2,128)(2,1)S(1)} all-to-all(bf16[4,2,16384]{2,1,0:T(2,128)(2,1)S(1)} %reshape.292), channel_id=1, replica_groups=mesh['facet'=4,'band'=4,'sub'=2] {'band'}, dimensions={0} | all-to-all | bytes 524288 | tf_op jit(solution)/shard_map/all_to_all | solution.py:92
  188.8 0.4 copy.29
  189.5 0.9 convolution_convert_fusion
  190.7 26.0 %all-gather.2.cloned.1.call-done = bf16[2,4,256,256]{3,2,1,0:T(8,128)(2,1)} async-done(((bf16[2,4,64,256]{3,2,1,0:T(8,128)(2,1)}), bf16[2,4,256,256]{3,2,1,0:T(8,128)(2,1)}) %all-gather.2.cloned.1.call-update) | async-done | bytes 1048592 | tf_op jit(solution)/shard_map/all_gather | solution.py:98
  216.7 11.7 %convolution_bitcast_fusion = f32[512,256]{1,0:T(8,128)S(1)} fusion(s32[4,256]{1,0:T(4,128)S(1)} %get-tuple-element.12, s32[512]{0:T(512)S(1)} %copy-done.4, s32[4,256]{1,0:T(4,128)S(1)} %get-tuple-element.13, bf16[2,4,256,256]{3,2,1,0:T(8,128)(2,1)} %all-gather.2.cloned.1.call-done), kind=kOutput, calls=%fused_computation.61 | convolution fusion | flops 282066944 | bytes 1058816 | tf_op jit(solution)/shard_map/gkx,gkl->xl/dot_general | solution.py:104
  228.4 10.8 %convolution_bitcast_fusion.2 = f32[512,256]{1,0:T(8,128)S(1)} fusion(s32[4,256]{1,0:T(4,128)S(1)} %get-tuple-element.12, s32[512]{0:T(512)S(1)} %copy-done.4, s32[4,256]{1,0:T(4,128)S(1)} %get-tuple-element.13, bf16[2,4,256,256]{3,2,1,0:T(8,128)(2,1)S(1)} %copy-done.9), kind=kOutput, calls=%fused_computation.63 | convolution fusion | flops 282066944 | bytes 1058816 | tf_op jit(solution)/shard_map/gkx,gkl->xl/dot_general | solution.py:100
  239.2 11.6 %fusion.40 = bf16[512,256]{1,0:T(8,128)(2,1)} fusion(f32[512,256]{1,0:T(8,128)S(1)} %convolution_bitcast_fusion, s32[4,256]{1,0:T(4,128)S(1)} %get-tuple-element.12, s32[512]{0:T(512)S(1)} %copy-done.4, s32[4,256]{1,0:T(4,128)S(1)} %get-tuple-element.13, bf16[2,4,256,256]{3,2,1,0:T(8,128)(2,1)S(1)} %copy-done.9), kind=kOutput, calls=%fused_computation.68 | convolution fusion | flops 282329088 | bytes 1320960 | tf_op jit(solution)/shard_map/gkx,gkl->xl/dot_general | solution.py:103
  250.7 11.4 %fusion.41 = bf16[512,256]{1,0:T(8,128)(2,1)} fusion(f32[512,256]{1,0:T(8,128)S(1)} %convolution_bitcast_fusion.2, s32[4,256]{1,0:T(4,128)S(1)} %get-tuple-element.12, s32[512]{0:T(512)S(1)} %copy-done.4, s32[4,256]{1,0:T(4,128)S(1)} %get-tuple-element.13, bf16[2,4,256,256]{3,2,1,0:T(8,128)(2,1)S(1)} %copy-done.9), kind=kOutput, calls=%fused_computation.69 | convolution fusion | flops 282329088 | bytes 1320960 | tf_op jit(solution)/shard_map/gkx,gkl->xl/dot_general | solution.py:99
  262.1 18.2 %all-reduce.6.cloned.1.call-done = (bf16[512,256]{1,0:T(8,128)(2,1)}, bf16[512,256]{1,0:T(8,128)(2,1)}) async-done(((bf16[512,256]{1,0:T(8,128)(2,1)}, bf16[512,256]{1,0:T(8,128)(2,1)}), (bf16[512,256]{1,0:T(8,128)(2,1)}, bf16[512,256]{1,0:T(8,128)(2,1)})) %all-reduce.6.cloned.1.call-update) | async-done | bytes 524304 | tf_op jit(solution)/shard_map/psum | solution.py:109
  280.4 11.8 %fusion.44 = f32[512,2048]{1,0:T(8,128)S(1)} fusion(bf16[512,256]{1,0:T(8,128)(2,1)} %get-tuple-element.5, s32[256]{0:T(256)S(1)} %copy-done.6, s32[2048]{0:T(1024)S(1)} %add_select_fusion.9, s32[256]{0:T(256)S(1)} %copy-done.8), kind=kOutput, calls=%fused_computation.77 | convolution fusion | flops 550502400 | bytes 4466688 | tf_op jit(solution)/shard_map/dot_general | solution.py:25
  292.1 12.3 %multiply_convert_fusion = bf16[512,2048]{1,0:T(8,128)(2,1)} fusion(f32[512,2048]{1,0:T(8,128)S(1)} %fusion.44, bf16[512,256]{1,0:T(8,128)(2,1)S(1)} %copy-done.10, f32[2048]{0:T(1024)S(1)} %copy-done.12, s32[256]{0:T(256)S(1)} %copy-done.6, s32[2048]{0:T(1024)S(1)} %add_select_fusion.9, s32[256]{0:T(256)S(1)} %copy-done.8), kind=kOutput, calls=%fused_computation | convolution fusion | flops 553648128 | bytes 6572032 | tf_op jit(solution)/shard_map/dot_general | solution.py:25
  (54 shorter events, 2.8 us)
Async XLA Ops:
  6.5 2.8 copy-start
  6.5 103.3 %reduce-scatter.2.cloned.1.call-start = ((), (), s32[]{:S(2)}) async-start(), calls=%async_computation.3 | async-start | bytes 1310720 | tf_op jit(solution)/shard_map/reduce_scatter | solution.py:65
  8.6 13.6 %copy-start.5 = (s32[256]{0:T(256)}, s32[256]{0:T(256)S(1)}, u32[]{:S(2)}) copy-start(s32[256]{0:T(256)S(1)} %get-tuple-element.14) | copy-start | bytes 3076
  8.6 13.6 %copy-start.7 = (s32[256]{0:T(256)}, s32[256]{0:T(256)S(1)}, u32[]{:S(2)}) copy-start(s32[256]{0:T(256)S(1)} %get-tuple-element.15) | copy-start | bytes 3076
  9.3 12.9 %copy-start.11 = (f32[2048]{0:T(1024)S(1)}, f32[2048]{0:T(1024)}, u32[]{:S(2)}) copy-start(f32[2048]{0:T(1024)} %param.8) | copy-start | bytes 24580
  22.3 11.1 %copy-start.13 = (s32[8]{0:T(128)S(1)}, s32[8]{0:T(128)}, u32[]{:S(2)}) copy-start(s32[8]{0:T(128)} %param.10) | copy-start | bytes 100
  33.4 33.1 %copy-start.3 = (s32[512]{0:T(512)}, s32[512]{0:T(512)S(1)}, u32[]{:S(2)}) copy-start(s32[512]{0:T(512)S(1)} %add_select_fusion.16) | copy-start | bytes 6148
  33.6 10.6 %copy-start.14 = (bf16[256,512]{1,0:T(8,128)(2,1)S(1)}, bf16[256,512]{1,0:T(8,128)(2,1)}, u32[]{:S(2)}) copy-start(bf16[256,512]{1,0:T(8,128)(2,1)} %convolution_convert_fusion.3) | copy-start | bytes 786436
  78.6 75.8 %copy-start.1 = (bf16[256,256]{1,0:T(8,128)(2,1)S(1)}, bf16[256,256]{1,0:T(8,128)(2,1)}, u32[]{:S(2)}) copy-start(bf16[256,256]{1,0:T(8,128)(2,1)} %param.12) | copy-start | bytes 393220
  79.7 82.0 %copy-start.2 = (s32[8,16,16]{2,1,0:T(8,128)S(1)}, s32[8,16,16]{2,1,0:T(8,128)}, u32[]{:S(2)}) copy-start(s32[8,16,16]{2,1,0:T(8,128)} %param.13) | copy-start | bytes 24580
  79.7 74.7 %all-reduce.4.cloned.1.call-start = ((), (), s32[]{:S(2)}) async-start(), calls=%async_computation.4 | async-start | bytes 524288 | tf_op jit(solution)/shard_map/psum | solution.py:68
  157.0 15.4 %all-to-all-start = ((bf16[4,2,16384]{2,1,0:T(2,128)(2,1)}), bf16[4,2,16384]{2,1,0:T(2,128)(2,1)S(1)}, u32[]{:S(2)}, u32[]{:S(2)}) async-start(bf16[4,2,16384]{2,1,0:T(2,128)(2,1)} %reshape.290), calls=%async_computation.1 | async-start | bytes 524288 | tf_op jit(solution)/shard_map/all_to_all | solution.py:83
  161.6 55.1 %all-gather.2.cloned.1.call-start = ((), (), s32[]{:S(2)}) async-start(), calls=%async_computation.5 | async-start | bytes 1310720 | tf_op jit(solution)/shard_map/all_gather | solution.py:98
  175.7 41.1 %copy-start.4 = (s32[512]{0:T(512)S(1)}, s32[512]{0:T(512)}, u32[]{:S(2)}) copy-start(s32[512]{0:T(512)} %copy-done.3) | copy-start | bytes 6148
  190.5 89.9 %all-reduce.6.cloned.1.call-start = ((), (), s32[]{:S(2)}) async-start(), calls=%async_computation.6 | async-start | bytes 1048576 | tf_op jit(solution)/shard_map/psum | solution.py:109
  216.7 11.7 %copy-start.9 = (bf16[2,4,256,256]{3,2,1,0:T(8,128)(2,1)S(1)}, bf16[2,4,256,256]{3,2,1,0:T(8,128)(2,1)}, u32[]{:S(2)}) copy-start(bf16[2,4,256,256]{3,2,1,0:T(8,128)(2,1)} %all-gather.2.cloned.1.call-done) | copy-start | bytes 3145732
  250.7 29.6 %copy-start.6 = (s32[256]{0:T(256)S(1)}, s32[256]{0:T(256)}, u32[]{:S(2)}) copy-start(s32[256]{0:T(256)} %copy-done.5) | copy-start | bytes 3076
  250.7 29.6 %copy-start.8 = (s32[256]{0:T(256)S(1)}, s32[256]{0:T(256)}, u32[]{:S(2)}) copy-start(s32[256]{0:T(256)} %copy-done.7) | copy-start | bytes 3076
  280.3 11.8 %copy-start.10 = (bf16[512,256]{1,0:T(8,128)(2,1)S(1)}, bf16[512,256]{1,0:T(8,128)(2,1)}, u32[]{:S(2)}) copy-start(bf16[512,256]{1,0:T(8,128)(2,1)} %get-tuple-element.6) | copy-start | bytes 786436
  280.3 11.8 %copy-start.12 = (f32[2048]{0:T(1024)S(1)}, f32[2048]{0:T(1024)}, u32[]{:S(2)}) copy-start(f32[2048]{0:T(1024)} %param.8) | copy-start | bytes 24580
Sparse Core Ops, SparseCore 0:
  79.8 29.9 reduce-scatter.1
  112.8 41.5 all-reduce.3
  190.6 26.0 all-gather.1
  262.3 18.0 all-reduce.5
where the time goes:
time: 316 us; the launch traced here: 311 us
  matrix products  141 us (45%)
  waiting for transfers between devices  119 us (38%)
  local copies, waits for them, and re-layouts  17.5 us (6%)
  between operations  15.1 us (5%)
  blocking collectives  12.7 us (4%)
  starting transfers between devices  4.85 us (2%)
    dot_general x6, matrix products, product(): return jnp.dot(left, right, preferred_element_type=jnp.float32)  69 us
    psum x1, waiting for transfers between devices, body(): blocks = lax.psum(blocks, 'facet')  44.5 us
    reduce_scatter x1, waiting for transfers between devices, body(): lax.psum_scatter(terms.astype(jnp.bfloat16), 'band', scatter_dimension=2,...  30.1 us
    all_gather x1, waiting for transfers between devices, body(): piece = lax.all_gather(residual_grid, 'band', axis=2, tiled=True)  26 us
    psum x1, waiting for transfers between devices, body(): lax.psum(e_real.astype(jnp.bfloat16), 'sub').astype(jnp.float32)  18.2 us
    dot_general x1, matrix products, body(): jnp.einsum('xy,ky->xk', facets, col_imag, preferred_element_type=jnp.floa...  12.9 us
    all_to_all x1, blocking collectives, body(): lax.all_to_all(u_cols, 'band', split_axis=3, concat_axis=2, tiled=True)  12.7 us
    dot_general x1, matrix products, body(): jnp.einsum('gkx,gkl->xl', back_imag, piece[0], preferred_element_type=jnp...  11.7 us
  transfers between devices with their start and end apart: 5, of which 4 were waited for; matrix products, arithmetic and copies ran while one was open for 3% of the time, Pallas kernels for 0%

commit v1 on v0

--- a/solution.py
+++ b/solution.py
@@ -65,7 +65,7 @@
     blocks = lax.psum_scatter(
         terms.astype(jnp.bfloat16), "band", scatter_dimension=2, tiled=True
     ).astype(jnp.float32)
-    blocks = lax.psum(blocks, "facet")
+    blocks = jnp.sum(lax.all_gather(blocks, "facet"), axis=0)
     grid_part = blocks.reshape(2, band_count, sub_rows, contrib).astype(jnp.bfloat16)
     tiles = tile_counts.shape[1]
     tile_side = contrib // tiles

time: 316 us -> 335 us (1.060)
  waiting for transfers between devices: 119 us -> 133 us
  other arithmetic: 0.95 us -> 6.15 us
    unnamed x4 -> x5, waiting for transfers between devices: 0.07 us -> 54.1 us
    psum x1 -> x0, waiting for transfers between devices: 44.5 us -> none  [body(): blocks = lax.psum(blocks, 'facet')]
    all_gather x0 -> x1, waiting for transfers between devices: none -> 34.6 us  [body(): blocks = jnp.sum(lax.all_gather(blocks, 'facet'), axis=0)]
    reduce_scatter x1 -> x0, waiting for transfers between devices: 30.1 us -> none  [body(): lax.psum_scatter(terms.astype(jnp.bfloat16), 'band', scatter_dimension=2,...]
where the time goes in v1:
time: 335 us; the launch traced here: 330 us
  matrix products  140 us (42%)
  waiting for transfers between devices  133 us (40%)
  local copies, waits for them, and re-layouts  17.2 us (5%)
  between operations  15.2 us (5%)
  blocking collectives  13 us (4%)
  other arithmetic  6.15 us (2%)
  starting transfers between devices  4.87 us (1%)
    dot_general x6, matrix products, product(): return jnp.dot(left, right, preferred_element_type=jnp.float32)  69 us
    unnamed x5, waiting for transfers between devices  54.1 us
    all_gather x1, waiting for transfers between devices, body(): blocks = jnp.sum(lax.all_gather(blocks, 'facet'), axis=0)  34.6 us
    all_gather x1, waiting for transfers between devices, body(): piece = lax.all_gather(residual_grid, 'band', axis=2, tiled=True)  26 us
    psum x1, waiting for transfers between devices, body(): lax.psum(e_real.astype(jnp.bfloat16), 'sub').astype(jnp.float32)  18.2 us
    all_to_all x1, blocking collectives, body(): lax.all_to_all(u_cols, 'band', split_axis=3, concat_axis=2, tiled=True)  13 us
    dot_general x1, matrix products, body(): jnp.einsum('xy,ky->xk', facets, col_imag, preferred_element_type=jnp.floa...  12.9 us
    dot_general x1, matrix products, body(): jnp.einsum('gkx,gkl->xl', back_imag, piece[0], preferred_element_type=jnp...  11.7 us
  transfers between devices with their start and end apart: 5, of which 4 were waited for; matrix products, arithmetic and copies ran while one was open for 3% of the time, Pallas kernels for 0%

profile of v1, /device:TPU:0, one launch (start us, length us, event | category | flops | bytes accessed | tf_op | source)
XLA Modules:
  0.0 329.7 jit_solution(7013215361662832762)
XLA Ops:
  7.3 0.8 constant_dynamic-slice_fusion
  8.1 0.6 fusion.137
  8.7 0.7 add_select_fusion.9
  9.4 12.9 %convolution_convert_fusion.3 = bf16[256,512]{1,0:T(8,128)(2,1)} fusion(bf16[512,2048]{1,0:T(8,128)(2,1)S(1)} %copy-done, f32[2048]{0:T(1024)} %param.8, s32[256]{0:T(256)S(1)} %get-tuple-element.14, s32[2048]{0:T(1024)S(1)} %add_select_fusion.9, s32[256]{0:T(256)S(1)} %get-tuple-element.15), kind=kOutput, calls=%fused_computation.73 | convolution fusion | flops 551682048 | bytes 2377728 | tf_op jit(solution)/shard_map/xy,ky->xk/dot_general | solution.py:53
  22.3 10.5 %convolution_convert_fusion.4 = bf16[256,512]{1,0:T(8,128)(2,1)S(1)} fusion(bf16[512,2048]{1,0:T(8,128)(2,1)S(1)} %copy-done, f32[2048]{0:T(1024)S(1)} %copy-done.11, s32[256]{0:T(256)S(1)} %get-tuple-element.14, s32[2048]{0:T(1024)S(1)} %add_select_fusion.9, s32[256]{0:T(256)S(1)} %get-tuple-element.15), kind=kOutput, calls=%fused_computation.74 | convolution fusion | flops 551157760 | bytes 2377728 | tf_op jit(solution)/shard_map/xy,ky->xk/dot_general | solution.py:50
  33.8 10.6 %fusion.58 = f32[1024,256]{1,0:T(8,128)S(1)} fusion(bf16[256,512]{1,0:T(8,128)(2,1)S(1)} %convolution_convert_fusion.4, s32[1024]{0:T(1024)S(1)} %get-tuple-element.8, s32[512]{0:T(512)S(1)} %add_select_fusion.16, s32[1024]{0:T(1024)S(1)} %get-tuple-element.7), kind=kOutput, calls=%fused_computation.88 | convolution fusion | flops 282066944 | bytes 1320960 | tf_op jit(solution)/shard_map/dot_general | solution.py:25
  44.4 10.7 %fusion.57 = f32[1024,256]{1,0:T(8,128)S(1)} fusion(bf16[256,512]{1,0:T(8,128)(2,1)S(1)} %copy-done.15, s32[1024]{0:T(1024)S(1)} %get-tuple-element.8, s32[512]{0:T(512)S(1)} %add_select_fusion.16, s32[1024]{0:T(1024)S(1)} %get-tuple-element.7), kind=kOutput, calls=%fused_computation.87 | convolution fusion | flops 282066944 | bytes 1320960 | tf_op jit(solution)/shard_map/dot_general | solution.py:25
  55.1 11.6 %fusion.36 = bf16[1024,256]{1,0:T(8,128)(2,1)S(1)} fusion(f32[1024,256]{1,0:T(8,128)S(1)} %fusion.58, bf16[256,512]{1,0:T(8,128)(2,1)S(1)} %copy-done.15, s32[1024]{0:T(1024)S(1)} %get-tuple-element.8, s32[512]{0:T(512)S(1)} %add_select_fusion.16, s32[1024]{0:T(1024)S(1)} %get-tuple-element.7), kind=kOutput, calls=%fused_computation.59 | convolution fusion | flops 283115520 | bytes 1845248 | tf_op jit(solution)/shard_map/dot_general | solution.py:25
  66.7 12.0 %fusion.37 = bf16[1024,256]{1,0:T(8,128)(2,1)S(1)} fusion(f32[1024,256]{1,0:T(8,128)S(1)} %fusion.57, bf16[256,512]{1,0:T(8,128)(2,1)S(1)} %convolution_convert_fusion.4, s32[1024]{0:T(1024)S(1)} %get-tuple-element.8, s32[512]{0:T(512)S(1)} %add_select_fusion.16, s32[1024]{0:T(1024)S(1)} %get-tuple-element.7), kind=kOutput, calls=%fused_computation.60 | convolution fusion | flops 283115520 | bytes 1845248 | tf_op jit(solution)/shard_map/dot_general | solution.py:25
  78.7 1.1 pad_maximum_fusion
  79.8 0.6 dynamic-slice
  80.5 54.1 %all-reduce.5.cloned.1.call-done = bf16[2,4,4,64,256]{4,3,2,1,0:T(8,128)(2,1)} async-done(((bf16[2,4,4,64,256]{4,3,2,1,0:T(8,128)(2,1)}), bf16[2,4,4,64,256]{4,3,2,1,0:T(8,128)(2,1)}) %all-reduce.5.cloned.1.call-update) | async-done | bytes 1048592
  134.6 2.4 dynamic-slice_convert_fusion
  137.0 34.6 %all-gather.6.cloned.1.call-done = f32[8,4,1,64,256]{4,3,2,1,0:T(8,128)} async-done(((f32[2,4,1,64,256]{4,3,2,1,0:T(8,128)}), f32[8,4,1,64,256]{4,3,2,1,0:T(8,128)}) %all-gather.6.cloned.1.call-update) | async-done | bytes 2097168 | tf_op jit(solution)/shard_map/all_gather | solution.py:68
  171.6 1.8 reduce.1
  174.0 1.1 reshape.297
  175.1 4.6 %all-to-all-start = ((bf16[4,2,16384]{2,1,0:T(2,128)(2,1)}), bf16[4,2,16384]{2,1,0:T(2,128)(2,1)S(1)}, u32[]{:S(2)}, u32[]{:S(2)}) async-start(bf16[4,2,16384]{2,1,0:T(2,128)(2,1)} %reshape.297), calls=%async_computation | async-start | bytes 524288 | tf_op jit(solution)/shard_map/all_to_all | solution.py:83
  179.8 3.9 %broadcast_in_dim.2 = f32[4,16,16,16,16]{2,1,4,3,0:T(8,128)} broadcast(f32[4,16,16]{1,2,0:T(8,128)S(1)} %copy.13), dimensions={0,1,3} | broadcast | bytes 1052672 | tf_op jit(solution)/shard_map/broadcast_in_dim | solution.py:76
  183.7 6.1 %reshape.285 = f32[4,256,256]{1,2,0:T(8,128)S(1)} reshape(f32[4,16,16,16,16]{2,1,4,3,0:T(8,128)} %broadcast_in_dim.2) | data formatting | bytes 2097152 | tf_op jit(solution)/shard_map/reshape | solution.py:79
  189.8 0.7 dynamic-slice_bitcast_fusion
  190.9 0.4 copy.25
  191.6 1.4 convolution_convert_fusion.1
  193.8 13.0 %all_to_all.36 = bf16[4,2,16384]{2,1,0:T(2,128)(2,1)S(1)} all-to-all(bf16[4,2,16384]{2,1,0:T(2,128)(2,1)S(1)} %reshape.299), channel_id=1, replica_groups=mesh['facet'=4,'band'=4,'sub'=2] {'band'}, dimensions={0} | all-to-all | bytes 524288 | tf_op jit(solution)/shard_map/all_to_all | solution.py:92
  207.9 0.9 convolution_convert_fusion
  209.1 26.0 %all-gather.4.cloned.1.call-done = bf16[2,4,256,256]{3,2,1,0:T(8,128)(2,1)} async-done(((bf16[2,4,64,256]{3,2,1,0:T(8,128)(2,1)}), bf16[2,4,256,256]{3,2,1,0:T(8,128)(2,1)}) %all-gather.4.cloned.1.call-update) | async-done | bytes 1048592 | tf_op jit(solution)/shard_map/all_gather | solution.py:98
  235.1 11.7 %convolution_bitcast_fusion = f32[512,256]{1,0:T(8,128)S(1)} fusion(s32[4,256]{1,0:T(4,128)S(1)} %get-tuple-element.12, s32[512]{0:T(512)S(1)} %copy-done.4, s32[4,256]{1,0:T(4,128)S(1)} %get-tuple-element.13, bf16[2,4,256,256]{3,2,1,0:T(8,128)(2,1)} %all-gather.4.cloned.1.call-done), kind=kOutput, calls=%fused_computation.61 | convolution fusion | flops 282066944 | bytes 1058816 | tf_op jit(solution)/shard_map/gkx,gkl->xl/dot_general | solution.py:104
  246.8 10.8 %convolution_bitcast_fusion.2 = f32[512,256]{1,0:T(8,128)S(1)} fusion(s32[4,256]{1,0:T(4,128)S(1)} %get-tuple-element.12, s32[512]{0:T(512)S(1)} %copy-done.4, s32[4,256]{1,0:T(4,128)S(1)} %get-tuple-element.13, bf16[2,4,256,256]{3,2,1,0:T(8,128)(2,1)S(1)} %copy-done.9), kind=kOutput, calls=%fused_computation.63 | convolution fusion | flops 282066944 | bytes 1058816 | tf_op jit(solution)/shard_map/gkx,gkl->xl/dot_general | solution.py:100
  257.6 11.6 %fusion.40 = bf16[512,256]{1,0:T(8,128)(2,1)} fusion(f32[512,256]{1,0:T(8,128)S(1)} %convolution_bitcast_fusion, s32[4,256]{1,0:T(4,128)S(1)} %get-tuple-element.12, s32[512]{0:T(512)S(1)} %copy-done.4, s32[4,256]{1,0:T(4,128)S(1)} %get-tuple-element.13, bf16[2,4,256,256]{3,2,1,0:T(8,128)(2,1)S(1)} %copy-done.9), kind=kOutput, calls=%fused_computation.68 | convolution fusion | flops 282329088 | bytes 1320960 | tf_op jit(solution)/shard_map/gkx,gkl->xl/dot_general | solution.py:103
  269.2 11.4 %fusion.41 = bf16[512,256]{1,0:T(8,128)(2,1)} fusion(f32[512,256]{1,0:T(8,128)S(1)} %convolution_bitcast_fusion.2, s32[4,256]{1,0:T(4,128)S(1)} %get-tuple-element.12, s32[512]{0:T(512)S(1)} %copy-done.4, s32[4,256]{1,0:T(4,128)S(1)} %get-tuple-element.13, bf16[2,4,256,256]{3,2,1,0:T(8,128)(2,1)S(1)} %copy-done.9), kind=kOutput, calls=%fused_computation.69 | convolution fusion | flops 282329088 | bytes 1320960 | tf_op jit(solution)/shard_map/gkx,gkl->xl/dot_general | solution.py:99
  280.5 18.2 %all-reduce.7.cloned.1.call-done = (bf16[512,256]{1,0:T(8,128)(2,1)}, bf16[512,256]{1,0:T(8,128)(2,1)}) async-done(((bf16[512,256]{1,0:T(8,128)(2,1)}, bf16[512,256]{1,0:T(8,128)(2,1)}), (bf16[512,256]{1,0:T(8,128)(2,1)}, bf16[512,256]{1,0:T(8,128)(2,1)})) %all-reduce.7.cloned.1.call-update) | async-done | bytes 524304 | tf_op jit(solution)/shard_map/psum | solution.py:109
  298.8 11.8 %fusion.44 = f32[512,2048]{1,0:T(8,128)S(1)} fusion(bf16[512,256]{1,0:T(8,128)(2,1)} %get-tuple-element.5, s32[256]{0:T(256)S(1)} %copy-done.6, s32[2048]{0:T(1024)S(1)} %add_select_fusion.9, s32[256]{0:T(256)S(1)} %copy-done.8), kind=kOutput, calls=%fused_computation.77 | convolution fusion | flops 550502400 | bytes 4466688 | tf_op jit(solution)/shard_map/dot_general | solution.py:25
  310.5 12.3 %multiply_convert_fusion = bf16[512,2048]{1,0:T(8,128)(2,1)} fusion(f32[512,2048]{1,0:T(8,128)S(1)} %fusion.44, bf16[512,256]{1,0:T(8,128)(2,1)S(1)} %copy-done.10, f32[2048]{0:T(1024)S(1)} %copy-done.12, s32[256]{0:T(256)S(1)} %copy-done.6, s32[2048]{0:T(1024)S(1)} %add_select_fusion.9, s32[256]{0:T(256)S(1)} %copy-done.8), kind=kOutput, calls=%fused_computation | convolution fusion | flops 553648128 | bytes 6572032 | tf_op jit(solution)/shard_map/dot_general | solution.py:25
  (58 shorter events, 3.7 us)
Async XLA Ops:
  6.5 2.8 copy-start
  6.5 128.0 %all-reduce.5.cloned.1.call-start = ((), (), s32[]{:S(2)}) async-start(), calls=%async_computation.4 | async-start | bytes 2097152
  8.7 13.6 %copy-start.5 = (s32[256]{0:T(256)}, s32[256]{0:T(256)S(1)}, u32[]{:S(2)}) copy-start(s32[256]{0:T(256)S(1)} %get-tuple-element.14) | copy-start | bytes 3076
  8.7 13.6 %copy-start.7 = (s32[256]{0:T(256)}, s32[256]{0:T(256)S(1)}, u32[]{:S(2)}) copy-start(s32[256]{0:T(256)S(1)} %get-tuple-element.15) | copy-start | bytes 3076
  9.4 12.9 %copy-start.11 = (f32[2048]{0:T(1024)S(1)}, f32[2048]{0:T(1024)}, u32[]{:S(2)}) copy-start(f32[2048]{0:T(1024)} %param.8) | copy-start | bytes 24580
  22.3 11.2 %copy-start.13 = (s32[8]{0:T(128)S(1)}, s32[8]{0:T(128)}, u32[]{:S(2)}) copy-start(s32[8]{0:T(128)} %param.10) | copy-start | bytes 100
  33.5 33.1 %copy-start.3 = (s32[512]{0:T(512)}, s32[512]{0:T(512)S(1)}, u32[]{:S(2)}) copy-start(s32[512]{0:T(512)S(1)} %add_select_fusion.16) | copy-start | bytes 6148
  33.7 10.6 %copy-start.15 = (bf16[256,512]{1,0:T(8,128)(2,1)S(1)}, bf16[256,512]{1,0:T(8,128)(2,1)}, u32[]{:S(2)}) copy-start(bf16[256,512]{1,0:T(8,128)(2,1)} %convolution_convert_fusion.3) | copy-start | bytes 786436
  78.6 1.2 copy-start.14
  79.8 93.6 %copy-start.1 = (bf16[256,256]{1,0:T(8,128)(2,1)S(1)}, bf16[256,256]{1,0:T(8,128)(2,1)}, u32[]{:S(2)}) copy-start(bf16[256,256]{1,0:T(8,128)(2,1)} %param.12) | copy-start | bytes 393220
  79.8 91.8 %all-gather.6.cloned.1.call-start = ((), (), s32[]{:S(2)}) async-start(), calls=%async_computation.3 | async-start | bytes 2621440 | tf_op jit(solution)/shard_map/all_gather | solution.py:68
  171.6 8.1 %copy-start.2 = (s32[8,16,16]{2,1,0:T(8,128)S(1)}, s32[8,16,16]{2,1,0:T(8,128)}, u32[]{:S(2)}) copy-start(s32[8,16,16]{2,1,0:T(8,128)} %param.13) | copy-start | bytes 24580
  175.1 15.4 %all-to-all-start = ((bf16[4,2,16384]{2,1,0:T(2,128)(2,1)}), bf16[4,2,16384]{2,1,0:T(2,128)(2,1)S(1)}, u32[]{:S(2)}, u32[]{:S(2)}) async-start(bf16[4,2,16384]{2,1,0:T(2,128)(2,1)} %reshape.297), calls=%async_computation | async-start | bytes 524288 | tf_op jit(solution)/shard_map/all_to_all | solution.py:83
  179.7 55.4 %all-gather.4.cloned.1.call-start = ((), (), s32[]{:S(2)}) async-start(), calls=%async_computation.2 | async-start | bytes 1310720 | tf_op jit(solution)/shard_map/all_gather | solution.py:98
  193.7 41.4 %copy-start.4 = (s32[512]{0:T(512)S(1)}, s32[512]{0:T(512)}, u32[]{:S(2)}) copy-start(s32[512]{0:T(512)} %copy-done.3) | copy-start | bytes 6148
  208.8 89.9 %all-reduce.7.cloned.1.call-start = ((), (), s32[]{:S(2)}) async-start(), calls=%async_computation.5 | async-start | bytes 1048576 | tf_op jit(solution)/shard_map/psum | solution.py:109
  235.1 11.7 %copy-start.9 = (bf16[2,4,256,256]{3,2,1,0:T(8,128)(2,1)S(1)}, bf16[2,4,256,256]{3,2,1,0:T(8,128)(2,1)}, u32[]{:S(2)}) copy-start(bf16[2,4,256,256]{3,2,1,0:T(8,128)(2,1)} %all-gather.4.cloned.1.call-done) | copy-start | bytes 3145732
  269.2 29.6 %copy-start.6 = (s32[256]{0:T(256)S(1)}, s32[256]{0:T(256)}, u32[]{:S(2)}) copy-start(s32[256]{0:T(256)} %copy-done.5) | copy-start | bytes 3076
  269.2 29.6 %copy-start.8 = (s32[256]{0:T(256)S(1)}, s32[256]{0:T(256)}, u32[]{:S(2)}) copy-start(s32[256]{0:T(256)} %copy-done.7) | copy-start | bytes 3076
  298.7 11.8 %copy-start.10 = (bf16[512,256]{1,0:T(8,128)(2,1)S(1)}, bf16[512,256]{1,0:T(8,128)(2,1)}, u32[]{:S(2)}) copy-start(bf16[512,256]{1,0:T(8,128)(2,1)} %get-tuple-element.6) | copy-start | bytes 786436
  298.7 11.8 %copy-start.12 = (f32[2048]{0:T(1024)S(1)}, f32[2048]{0:T(1024)}, u32[]{:S(2)}) copy-start(f32[2048]{0:T(1024)} %param.8) | copy-start | bytes 24580
Sparse Core Ops, SparseCore 0:
  79.9 54.6 all-reduce.4
  137.1 34.4 all-gather.5
  209.0 26.1 all-gather.3
  280.7 18.0 all-reduce.6
